TPU v7x, 256 devices: a whole 4x4x8 slice. The times are simulated.
256 devices in a mesh: section: 16 (over y_hi, x, core), ray: 8 (over z), dp: 2 (over y_lo).
Axes of the slice: x: 4, y: 4 (y_hi: 2, y_lo: 2; y = y_hi * 2 + y_lo), z: 8, core: 2. Of those that a mesh axis runs over, the one named last changes fastest.
Arguments:
- section_tokens: bfloat16 [16, 2, 1024, 1024], P('section', 'dp', 'ray'), may hold values from -6 to 6
- enc_ln1: float32 [16, 1024], P('section'), may hold values from 0.5 to 1.5
- enc_qkv: bfloat16 [16, 1024, 3, 1024], P('section', None, None, 'ray'), may hold values from -40 to 40
- enc_out: bfloat16 [16, 1024, 1024], P('section', 'ray'), may hold values from -0.1875 to 0.1875
- enc_ln2: float32 [16, 1024], P('section'), may hold values from 0.5 to 1.5
- enc_up: bfloat16 [16, 1024, 4096], P('section', None, 'ray'), may hold values from -0.1875 to 0.1875
- enc_down: bfloat16 [16, 4096, 1024], P('section', 'ray'), may hold values from -0.09375 to 0.09375
- set_latent: bfloat16 [2, 1024, 1024], P('dp', 'ray'), may hold values from -6 to 6
- ray_queries: bfloat16 [2, 32768, 1024], P('dp', ('section', 'ray')), may hold values from -6 to 6
- dec_query: bfloat16 [1024, 1024], P('section'), may hold values from -40 to 40
- dec_kv: bfloat16 [1024, 2, 1024], P('section'), may hold values from -1 to 1
- dec_out: bfloat16 [1024, 1024], P('section'), may hold values from -0.1875 to 0.1875
- feature_grad: bfloat16 [2, 32768, 1024], P('dp', ('section', 'ray')), may hold values from -2 to 2
Outputs:
- handed: bfloat16 [16, 2, 1024, 1024], P('section', 'dp', 'ray')
- finished: bfloat16 [2, 1024, 1024], P('dp', 'ray', 'section')
- ray_features: bfloat16 [2, 32768, 1024], P('dp', ('section', 'ray'))
- latent_grad: bfloat16 [2, 1024, 1024], P('dp', 'ray')
- out_grad: float32 [1024, 1024], replicated
All inputs are finite; a program needn't handle non-finite values.
Results may differ from a plain program's by a relative error of at most 0.022.
The roundings to bfloat16 on the way count: a program that leaves them out, or rounds other values in their place, can miss the bound.
Values may be sent and summed in bfloat16 or wider, within the bound.
No kernel may reach another device: no remote copies, remote signals or barrier semaphores. Data moves between devices by JAX's collectives and lax.ppermute only.
A program may use at most 128 MiB of HBM per device.

v0:
```python
import math
import jax
import jax.numpy as jnp
from jax import lax
from jax.sharding import PartitionSpec as P

HEADS = 16


def shifted(value, axis, by):
    count = lax.axis_size(axis)
    pairs = [(i, i + by) for i in range(count) if 0 <= i + by < count]
    return lax.ppermute(value, axis, pairs)


def spread_2(value, axis, root):
    mine = lax.axis_index(axis) == root
    return lax.psum(jnp.where(mine, value, jnp.zeros_like(value)), axis)


def layer_norm(values, gain):
    values = values.astype(jnp.float32)
    center = values - jnp.mean(values, -1, keepdims=True)
    spread = jnp.mean(center * center, -1, keepdims=True)
    return center * lax.rsqrt(spread + 1e-05) * gain


def softmax_rows(scores):
    top = jnp.max(scores, -1, keepdims=True)
    expo = jnp.exp(scores - top)
    return expo / jnp.sum(expo, -1, keepdims=True)


def attend_heads(packed, head_dim):
    length = packed.shape[0]
    heads = packed.shape[1] // (3 * head_dim)
    split = packed.reshape(length, 3, heads, head_dim)
    scores = jnp.einsum(
        "qhd,khd->hqk", split[:, 0], split[:, 1], preferred_element_type=jnp.float32
    ) / math.sqrt(head_dim)
    probs = softmax_rows(scores).astype(jnp.bfloat16)
    mixed = jnp.einsum("hqk,khd->qhd", probs, split[:, 2], preferred_element_type=jnp.float32)
    return mixed.astype(jnp.bfloat16).reshape(length, heads * head_dim)


def latent_rows(pair_sum, w_pairs):
    result = lax.dot_general(
        pair_sum[:, 0],
        w_pairs[:, 0, :],
        (((1,), (1,)), ((), ())),
        preferred_element_type=jnp.float32,
    )
    result = result + lax.dot_general(
        pair_sum[:, 1],
        w_pairs[:, 1, :],
        (((1,), (1,)), ((), ())),
        preferred_element_type=jnp.float32,
    )
    return result.astype(jnp.bfloat16)


def local(
    section_tokens,
    enc_ln1,
    enc_qkv,
    enc_out,
    enc_ln2,
    enc_up,
    enc_down,
    set_latent,
    ray_queries,
    dec_query,
    dec_kv,
    dec_out,
    feature_grad,
):
    tokens = section_tokens[0, 0]
    width = tokens.shape[1]
    head_dim = width // HEADS
    local_width = enc_out.shape[1]
    w_qkv = enc_qkv[0].reshape(width, 3 * local_width)
    w_attn_out = enc_out[0]
    w_upper = enc_up[0]
    w_lower = enc_down[0]
    gain_one = enc_ln1[0]
    gain_two = enc_ln2[0]
    normed = layer_norm(tokens, gain_one).astype(jnp.bfloat16)
    packed = jnp.dot(
        lax.all_gather(normed, "ray", axis=0, tiled=True), w_qkv, preferred_element_type=jnp.float32
    ).astype(jnp.bfloat16)
    mixed = attend_heads(packed, head_dim)
    attn_rows = lax.psum_scatter(
        jnp.dot(mixed, w_attn_out, preferred_element_type=jnp.float32).astype(jnp.bfloat16),
        "ray",
        scatter_dimension=0,
        tiled=True,
    ).astype(jnp.float32)
    hidden = (tokens.astype(jnp.float32) + attn_rows).astype(jnp.bfloat16)
    upper = jax.nn.gelu(
        jnp.dot(
            lax.all_gather(
                layer_norm(hidden, gain_two).astype(jnp.bfloat16), "ray", axis=0, tiled=True
            ),
            w_upper,
            preferred_element_type=jnp.float32,
        ),
        approximate=True,
    ).astype(jnp.bfloat16)
    lower_rows = lax.psum_scatter(
        jnp.dot(upper, w_lower, preferred_element_type=jnp.float32).astype(jnp.bfloat16),
        "ray",
        scatter_dimension=0,
        tiled=True,
    ).astype(jnp.float32)
    layer_out = (hidden.astype(jnp.float32) + lower_rows).astype(jnp.bfloat16)
    handed = shifted(layer_out, "section", 1)
    finished_all = spread_2(layer_out, "section", lax.axis_size("section") - 1)
    columns = width // lax.axis_size("section")
    finished = lax.dynamic_slice_in_dim(
        finished_all, lax.axis_index("section") * columns, columns, 1
    )
    w_query, w_pairs, w_mix = (
        lax.all_gather(dec_query, "section", axis=0, tiled=True),
        lax.all_gather(dec_kv, "section", axis=0, tiled=True),
        lax.all_gather(dec_out, "section", axis=0, tiled=True),
    )
    latent = set_latent[0]
    queries = ray_queries[0]
    cotangent = feature_grad[0]
    flat_pairs = w_pairs.reshape(width, 2 * width)
    key_values = lax.all_gather(
        jnp.dot(latent, flat_pairs, preferred_element_type=jnp.float32).astype(jnp.bfloat16),
        "ray",
        axis=0,
        tiled=True,
    )
    scene_len = key_values.shape[0]
    ray_rows = queries.shape[0]
    scale = 1.0 / math.sqrt(head_dim)
    keys = key_values[:, :width].reshape(scene_len, HEADS, head_dim)
    values = key_values[:, width:].reshape(scene_len, HEADS, head_dim)
    query = (
        jnp.dot(queries, w_query, preferred_element_type=jnp.float32)
        .astype(jnp.bfloat16)
        .reshape(ray_rows, HEADS, head_dim)
    )
    scores = jnp.einsum("rhd,lhd->hrl", query, keys, preferred_element_type=jnp.float32) * scale
    probs = softmax_rows(scores)
    probs_low = probs.astype(jnp.bfloat16)
    attended = (
        jnp.einsum("hrl,lhd->rhd", probs_low, values, preferred_element_type=jnp.float32)
        .astype(jnp.bfloat16)
        .reshape(ray_rows, width)
    )
    features = (
        queries.astype(jnp.float32) + jnp.dot(attended, w_mix, preferred_element_type=jnp.float32)
    ).astype(jnp.bfloat16)
    mix_term = lax.dot_general(
        attended, cotangent, (((0,), (0,)), ((), ())), preferred_element_type=jnp.float32
    )
    out_grad = lax.psum(mix_term, ("section", "ray", "dp"))
    attn_grad = lax.dot_general(
        cotangent, w_mix, (((1,), (1,)), ((), ())), preferred_element_type=jnp.float32
    )
    attn_grad = attn_grad.astype(jnp.bfloat16).reshape(ray_rows, HEADS, head_dim)
    prob_grad = jnp.einsum("rhd,lhd->hrl", attn_grad, values, preferred_element_type=jnp.float32)
    delta = jnp.sum(probs * prob_grad, -1, keepdims=True)
    score_grad = (probs * (prob_grad - delta) * scale).astype(jnp.bfloat16)
    count = latent.shape[0] * lax.axis_size("ray")
    key_grad = jnp.einsum(
        "hrl,rhd->lhd", score_grad, query, preferred_element_type=jnp.float32
    ).reshape(count, width)
    value_grad = jnp.einsum(
        "hrl,rhd->lhd", probs_low, attn_grad, preferred_element_type=jnp.float32
    ).reshape(count, width)
    stacked = jnp.stack([key_grad, value_grad], 1)
    pair_rows = lax.psum_scatter(
        stacked.astype(jnp.bfloat16), "ray", scatter_dimension=0, tiled=True
    )
    pair_sum = lax.psum(pair_rows, "section")
    latent_grad = latent_rows(pair_sum, w_pairs)
    return (handed[None, None], finished[None], features[None], latent_grad[None], out_grad)


def solution(mesh):
    return jax.shard_map(
        local,
        mesh=mesh,
        in_specs=(
            P("section", "dp", "ray", None),
            P("section", None),
            P("section", None, None, "ray"),
            P("section", "ray", None),
            P("section", None),
            P("section", None, "ray"),
            P("section", "ray", None),
            P("dp", "ray", None),
            P("dp", ("section", "ray"), None),
            P("section", None),
            P("section", None, None),
            P("section", None),
            P("dp", ("section", "ray"), None),
        ),
        out_specs=(
            P("section", "dp", "ray", None),
            P("dp", "ray", "section"),
            P("dp", ("section", "ray"), None),
            P("dp", "ray", None),
            P(),
        ),
        check_vma=False,
    )
```

profile of v0, /device:TPU:2, one launch (start us, length us, event | category | flops | bytes accessed | tf_op | source)
XLA Modules:
  0.0 928.3 jit_solution(4946242236666145838)
XLA Ops:
  8.1 1.1 convert_reduce_fusion.1
  9.2 1.2 fusion.73
  10.4 1.9 fusion.75
  12.4 1.4 copy.44
  13.8 42.5 %all-gather.7.cloned.1.call-done = bf16[1024,1024]{1,0:T(8,128)(2,1)} async-done(((bf16[128,1024]{1,0:T(8,128)(2,1)}), bf16[1024,1024]{1,0:T(8,128)(2,1)}) %all-gather.7.cloned.1.call-update) | async-done | bytes 2097168 | tf_op jit(solution)/shard_map/all_gather | solution.py:89
  56.3 2.6 convolution_convert_fusion.3
  58.9 4.9 fusion.97
  63.7 4.3 fusion.48
  68.1 2.1 convolution_convert_fusion.2
  71.9 39.7 %reduce-scatter.6.cloned.1.call-done = bf16[128,1024]{1,0:T(8,128)(2,1)} async-done(((bf16[1024,1024]{1,0:T(8,128)(2,1)}), bf16[128,1024]{1,0:T(8,128)(2,1)}) %reduce-scatter.6.cloned.1.call-update) | async-done | bytes 262160 | tf_op jit(solution)/shard_map/reduce_scatter | solution.py:92
  111.7 1.1 convert_reduce_fusion
  113.0 0.9 fusion.72
  114.0 18.6 %all-gather.11.cloned.1.call-done = bf16[1024,2,1024]{2,1,0:T(2,128)(2,1)} async-done(((bf16[64,2,1024]{2,1,0:T(2,128)(2,1)}), bf16[1024,2,1024]{2,1,0:T(2,128)(2,1)}) %all-gather.11.cloned.1.call-update) | async-done | bytes 4194320 | tf_op jit(solution)/shard_map/all_gather | solution.py:124
  132.7 11.1 %copy.47 = bf16[1024,2,1024]{0,2,1:T(8,128)(2,1)} copy(bf16[1024,2,1024]{2,1,0:T(2,128)(2,1)} %all-gather.11.cloned.1.call-done) | data formatting | bytes 8388608 | tf_op jit(solution)/shard_map/all_gather | solution.py:124
  143.8 4.6 convolution_convert_fusion
  148.5 39.0 %all-gather.15.cloned.1.call-done = bf16[1024,1024]{1,0:T(8,128)(2,1)} async-done(((bf16[64,1024]{1,0:T(8,128)(2,1)}), bf16[1024,1024]{1,0:T(8,128)(2,1)}) %all-gather.15.cloned.1.call-update) | async-done | bytes 2097168 | tf_op jit(solution)/shard_map/all_gather | solution.py:123
  187.5 2.3 convolution_convert_fusion.5
  189.8 1.0 copy.49
  190.8 51.5 %all-gather.17.cloned.1.call-done = bf16[1024,1024]{1,0:T(8,128)(2,1)} async-done(((bf16[64,1024]{1,0:T(8,128)(2,1)}), bf16[1024,1024]{1,0:T(8,128)(2,1)}) %all-gather.17.cloned.1.call-update) | async-done | bytes 2097168 | tf_op jit(solution)/shard_map/all_gather | solution.py:125
  242.3 2.3 convolution_convert_fusion.4
  244.6 1.0 copy.51
  245.6 39.2 %all-gather.9.cloned.1.call-done = bf16[1024,1024]{1,0:T(8,128)(2,1)} async-done(((bf16[128,1024]{1,0:T(8,128)(2,1)}), bf16[1024,1024]{1,0:T(8,128)(2,1)}) %all-gather.9.cloned.1.call-update) | async-done | bytes 2097168 | tf_op jit(solution)/shard_map/all_gather | solution.py:101
  284.9 5.8 convolution_convert_fusion.1
  290.9 66.2 %all-gather.13.cloned.1.call-done = bf16[1024,2048]{1,0:T(8,128)(2,1)} async-done(((bf16[128,2048]{1,0:T(8,128)(2,1)}), bf16[1024,2048]{1,0:T(8,128)(2,1)}) %all-gather.13.cloned.1.call-update) | async-done | bytes 4194320 | tf_op jit(solution)/shard_map/all_gather | solution.py:131
  357.2 4.0 fusion.96
  361.2 2.6 copy.50
  363.8 2.9 copy.48
  366.7 9.8 %fusion.98 = (f32[16,256]{1,0:T(8,128)S(1)}, f32[16,256,1024]{2,1,0:T(8,128)}) fusion(bf16[256,16,64]{0,2,1:T(8,128)(2,1)S(1)} %bitcast.149, bf16[1024,16,64]{0,2,1:T(8,128)(2,1)} %bitcast.144), kind=kOutput, calls=%fused_computation.110 | convolution fusion | flops 549454848 | bytes 19415040 | tf_op jit(solution)/shard_map/sub | solution.py:30
  376.5 8.1 fusion.99
  384.5 38.2 %fusion.38 = bf16[16,64,1024]{2,1,0:T(8,128)(2,1)} fusion(bf16[256,16,64]{0,2,1:T(8,128)(2,1)S(1)} %bitcast.150, f32[16,256,1024]{2,1,0:T(8,128)} %fusion.99, f32[16,256,1024]{2,1,0:T(8,128)} %get-tuple-element.18, f32[16,256]{1,0:T(8,128)S(1)} %get-tuple-element.17), kind=kOutput, calls=%fused_computation.40 | convolution fusion | flops 567284736 | bytes 36192256 | tf_op jit(solution)/shard_map/hrl,rhd->lhd/dot_general | solution.py:170
  422.8 7.1 fusion.35
  429.9 2.4 pad_maximum_fusion
  432.3 6.5 copy.57
  438.9 1.9 broadcast_select_fusion
  440.8 52.2 %reduce-scatter.10.cloned.1.call-done = bf16[128,2048]{1,0:T(8,128)(2,1)} async-done(((bf16[1024,2048]{1,0:T(8,128)(2,1)}), bf16[128,2048]{1,0:T(8,128)(2,1)}) %reduce-scatter.10.cloned.1.call-update) | async-done | bytes 524304
  492.9 2.0 copy.58
  495.3 8.5 fusion.42
  503.8 2.7 fusion.78
  506.5 10.0 %fusion.95 = (bf16[1024,1,1024]{2,1,0:T(2,128)(2,1)}, bf16[1024,1,1024]{2,1,0:T(2,128)(2,1)}) fusion(bf16[1024,2,1024]{2,1,0:T(2,128)(2,1)} %all-gather.11.cloned.1.call-done), kind=kLoop, calls=%fused_computation.107 | loop fusion | bytes 8388608 | tf_op jit(solution)/shard_map/slice | solution.py:49
  516.5 1.9 collective-permute-start
  518.5 1.5 fusion.45
  520.0 4.7 collective-permute-done
  524.7 109.9 %all-reduce.6.cloned.1.call-done = (bf16[128,1024]{1,0:T(8,128)(2,1)}, bf16[128,2,1024]{0,2,1:T(8,128)(2,1)}) async-done(((bf16[128,1024]{1,0:T(8,128)(2,1)}, bf16[128,2,1024]{0,2,1:T(8,128)(2,1)}), (bf16[128,1024]{1,0:T(8,128)(2,1)}, bf16[128,2,1024]{0,2,1:T(8,128)(2,1)})) %all-reduce.6.cloned.1.call-update) | async-done | bytes 786448 | tf_op jit(solution)/shard_map/psum | solution.py:18
  634.6 0.8 constant_dynamic-slice_fusion
  636.2 3.1 fusion.33
  639.3 3.9 fusion.49
  643.2 272.5 %all-reduce.4.cloned.1.call-done = f32[1024,1024]{1,0:T(8,128)} async-done(((f32[1024,1024]{1,0:T(8,128)}), f32[1024,1024]{1,0:T(8,128)}) %all-reduce.4.cloned.1.call-update) | async-done | bytes 4194320 | tf_op jit(solution)/shard_map/psum | solution.py:161
  916.4 4.8 copy.76
  (60 shorter events, 4.3 us)
Async XLA Ops:
  8.0 276.9 %copy-start = (bf16[1,512,1024]{2,1,0:T(8,128)(2,1)S(1)}, bf16[1,512,1024]{2,1,0:T(8,128)(2,1)}, u32[]{:S(2)}) copy-start(bf16[1,512,1024]{2,1,0:T(8,128)(2,1)} %param.19) | copy-start | bytes 3145732
  8.0 48.2 %all-gather.7.cloned.1.call-start = ((), (), s32[]{:S(2)}) async-start(), calls=%async_computation.3 | async-start | bytes 2359296 | tf_op jit(solution)/shard_map/all_gather | solution.py:89
  12.3 99.4 %reduce-scatter.6.cloned.1.call-start = ((), (), s32[]{:S(2)}) async-start(), calls=%async_computation.4 | async-start | bytes 2359296 | tf_op jit(solution)/shard_map/reduce_scatter | solution.py:92
  63.7 4.3 copy-start.11
  68.0 43.6 %copy-start.2 = (bf16[1,1,128,1024]{3,2,1,0:T(8,128)(2,1)S(1)}, bf16[1,1,128,1024]{3,2,1,0:T(8,128)(2,1)}, u32[]{:S(2)}) copy-start(bf16[1,1,128,1024]{3,2,1,0:T(8,128)(2,1)} %param.13) | copy-start | bytes 786436
  68.0 45.0 %copy-start.14 = (f32[1,1024]{1,0:T(1,128)S(1)}, f32[1,1024]{1,0:T(1,128)}, u32[]{:S(2)}) copy-start(f32[1,1024]{1,0:T(1,128)} %param.17) | copy-start | bytes 12292
  70.1 62.5 %all-gather.11.cloned.1.call-start = ((), (), s32[]{:S(2)}) async-start(), calls=%async_computation.7 | async-start | bytes 4456448 | tf_op jit(solution)/shard_map/all_gather | solution.py:124
  70.7 116.8 %all-gather.15.cloned.1.call-start = ((), (), s32[]{:S(2)}) async-start(), calls=%async_computation.9 | async-start | bytes 2228224 | tf_op jit(solution)/shard_map/all_gather | solution.py:123
  71.3 171.0 %all-gather.17.cloned.1.call-start = ((), (), s32[]{:S(2)}) async-start(), calls=%async_computation.10 | async-start | bytes 2228224 | tf_op jit(solution)/shard_map/all_gather | solution.py:125
  71.9 213.0 %all-gather.9.cloned.1.call-start = ((), (), s32[]{:S(2)}) async-start(), calls=%async_computation.5 | async-start | bytes 2359296 | tf_op jit(solution)/shard_map/all_gather | solution.py:101
  114.0 29.8 %copy-start.12 = (bf16[1,128,1024]{2,1,0:T(8,128)(2,1)S(1)}, bf16[1,128,1024]{2,1,0:T(8,128)(2,1)}, u32[]{:S(2)}) copy-start(bf16[1,128,1024]{2,1,0:T(8,128)(2,1)} %param.20) | copy-start | bytes 786436
  114.0 243.2 %all-gather.13.cloned.1.call-start = ((), (), s32[]{:S(2)}) async-start(), calls=%async_computation.8 | async-start | bytes 4718592 | tf_op jit(solution)/shard_map/all_gather | solution.py:131
  143.8 43.7 %copy-start.8 = (bf16[1,256,1024]{2,1,0:T(8,128)(2,1)S(1)}, bf16[1,256,1024]{2,1,0:T(8,128)(2,1)}, u32[]{:S(2)}) copy-start(bf16[1,256,1024]{2,1,0:T(8,128)(2,1)} %param.21) | copy-start | bytes 1572868
  143.8 98.5 %copy-start.6 = (bf16[1,256,1024]{2,1,0:T(8,128)(2,1)S(1)}, bf16[1,256,1024]{2,1,0:T(8,128)(2,1)}, u32[]{:S(2)}) copy-start(bf16[1,256,1024]{2,1,0:T(8,128)(2,1)} %param.25) | copy-start | bytes 1572868
  148.5 290.5 %reduce-scatter.8.cloned.1.call-start = ((), (), s32[]{:S(2)}) async-start(), calls=%async_computation.6 | async-start | bytes 2359296 | tf_op jit(solution)/shard_map/reduce_scatter | solution.py:109
  290.7 202.2 %reduce-scatter.10.cloned.1.call-start = ((), (), s32[]{:S(2)}) async-start(), calls=%async_computation.12 | async-start | bytes 4718592
  361.2 5.4 copy-start.10
  366.6 9.8 %copy-start.4 = (bf16[256,1024]{0,1:T(8,128)(2,1)S(1)}, bf16[256,1024]{0,1:T(8,128)(2,1)}, u32[]{:S(2)}) copy-start(bf16[256,1024]{0,1:T(8,128)(2,1)} %copy.51) | copy-start | bytes 1572868
  422.8 7.1 copy-start.5
  438.8 195.8 %all-reduce.6.cloned.1.call-start = ((), (), s32[]{:S(2)}) async-start(), calls=%async_computation.13 | async-start | bytes 1572864 | tf_op jit(solution)/shard_map/psum | solution.py:18
  495.0 8.8 copy-start.7
  495.0 420.7 %all-reduce.4.cloned.1.call-start = ((), (), s32[]{:S(2)}) async-start(), calls=%async_computation.11 | async-start | bytes 8388608 | tf_op jit(solution)/shard_map/psum | solution.py:161
  506.5 10.0 %copy-start.13 = (bf16[128,1024]{1,0:T(8,128)(2,1)S(1)}, bf16[128,1024]{1,0:T(8,128)(2,1)}, u32[]{:S(2)}) copy-start(bf16[128,1024]{1,0:T(8,128)(2,1)} %get-tuple-element.8) | copy-start | bytes 786436
  506.5 11.9 %copy-start.3 = (bf16[1024,1024]{1,0:T(8,128)(2,1)S(1)}, bf16[1024,1024]{1,0:T(8,128)(2,1)}, u32[]{:S(2)}) copy-start(bf16[1024,1024]{1,0:T(8,128)(2,1)} %all-gather.17.cloned.1.call-done) | copy-start | bytes 6291460
  506.5 11.9 %copy-start.9 = (bf16[1,256,1024]{2,1,0:T(8,128)(2,1)S(1)}, bf16[1,256,1024]{2,1,0:T(8,128)(2,1)}, u32[]{:S(2)}) copy-start(bf16[1,256,1024]{2,1,0:T(8,128)(2,1)} %param.21) | copy-start | bytes 1572868
  516.5 8.2 collective-permute-start
  915.7 5.5 copy-start.1
Sparse Core Ops, SparseCore 0:
  12.4 43.7 all-gather.6
  70.3 41.3 reduce-scatter.5
  290.8 69.1 reduce-scatter.7
  439.0 53.9 reduce-scatter.9
Sparse Core Ops, SparseCore 1:
  73.4 59.3 all-gather.10
  135.3 52.1 all-gather.14
  190.1 52.1 all-gather.16
  244.7 40.1 all-gather.8
  286.7 70.4 all-gather.12
  495.1 139.5 all-reduce.5
  640.0 275.7 all-reduce.3
where the time goes:
time: 929 us; the launch traced here: 928 us
  waiting for transfers between devices  738 us (79%)
  matrix products  112 us (12%)
  local copies, waits for them, and re-layouts  49.6 us (5%)
  between operations  15.6 us (2%)
  other arithmetic  10.7 us (1%)
    psum x1, waiting for transfers between devices, local(): out_grad = lax.psum(mix_term, ('section', 'ray', 'dp'))  273 us
    psum x1, waiting for transfers between devices, spread_2(): return lax.psum(jnp.where(mine, value, jnp.zeros_like(value)), axis)  110 us
    all_gather x1, waiting for transfers between devices, local(): lax.all_gather(jnp.dot(latent, flat_pairs, preferred_element_type=jnp.flo...  66.2 us
    unnamed x12, waiting for transfers between devices  53.9 us
    all_gather x1, waiting for transfers between devices, local(): lax.all_gather(dec_out, 'section', axis=0, tiled=True)  51.5 us
    all_gather x1, waiting for transfers between devices, local(): lax.all_gather(normed, 'ray', axis=0, tiled=True)  42.5 us
    reduce_scatter x1, waiting for transfers between devices, local(): lax.psum_scatter(jnp.dot(mixed, w_attn_out, preferred_element_type=jnp.fl...  39.7 us
    all_gather x1, waiting for transfers between devices, local(): lax.all_gather(layer_norm(hidden, gain_two).astype(jnp.bfloat16), 'ray',...  39.2 us
  transfers between devices with their start and end apart: 12, of which 11 were waited for; matrix products, arithmetic and copies ran while one was open for 16% of the time, Pallas kernels for 0%

commit v1 on v0

--- a/solution.py
+++ b/solution.py
@@ -158,7 +158,7 @@
     mix_term = lax.dot_general(
         attended, cotangent, (((0,), (0,)), ((), ())), preferred_element_type=jnp.float32
     )
-    out_grad = lax.psum(mix_term, ("section", "ray", "dp"))
+    out_grad = lax.psum(lax.psum(mix_term, "section"), ("ray", "dp"))
     attn_grad = lax.dot_general(
         cotangent, w_mix, (((1,), (1,)), ((), ())), preferred_element_type=jnp.float32
     )

time: 929 us -> 972 us (1.046)
  waiting for transfers between devices: 738 us -> 780 us
    psum x1 -> x2, waiting for transfers between devices: 273 us -> 305 us  [local(): out_grad = lax.psum(lax.psum(mix_term, 'section'), ('ray', 'dp'))]
    psum x1, waiting for transfers between devices: 110 us -> 129 us  [spread_2(): return lax.psum(jnp.where(mine, value, jnp.zeros_like(value)), axis)]
    unnamed x12 -> x13, waiting for transfers between devices: 53.9 us -> 42.4 us
  transfers between devices with their start and end apart: 12 -> 13, of which waited for: 11 -> 12; matrix products, arithmetic and copies ran while one was open for 16% -> 15% of each run, Pallas kernels for 0% -> 0%
where the time goes in v1:
time: 972 us; the launch traced here: 971 us
  waiting for transfers between devices  780 us (80%)
  matrix products  112 us (12%)
  local copies, waits for them, and re-layouts  49.6 us (5%)
  between operations  15.6 us (2%)
  other arithmetic  10.6 us (1%)
    psum x2, waiting for transfers between devices, local(): out_grad = lax.psum(lax.psum(mix_term, 'section'), ('ray', 'dp'))  305 us
    psum x1, waiting for transfers between devices, spread_2(): return lax.psum(jnp.where(mine, value, jnp.zeros_like(value)), axis)  129 us
    all_gather x1, waiting for transfers between devices, local(): lax.all_gather(jnp.dot(latent, flat_pairs, preferred_element_type=jnp.flo...  66.3 us
    all_gather x1, waiting for transfers between devices, local(): lax.all_gather(dec_out, 'section', axis=0, tiled=True)  51.5 us
    all_gather x1, waiting for transfers between devices, local(): lax.all_gather(normed, 'ray', axis=0, tiled=True)  42.5 us
    unnamed x13, waiting for transfers between devices  42.4 us
    reduce_scatter x1, waiting for transfers between devices, local(): lax.psum_scatter(jnp.dot(mixed, w_attn_out, preferred_element_type=jnp.fl...  39.8 us
    all_gather x1, waiting for transfers between devices, local(): lax.all_gather(layer_norm(hidden, gain_two).astype(jnp.bfloat16), 'ray',...  39.2 us
  transfers between devices with their start and end apart: 13, of which 12 were waited for; matrix products, arithmetic and copies ran while one was open for 15% of the time, Pallas kernels for 0%

profile of v1, /device:TPU:2, one launch (start us, length us, event | category | flops | bytes accessed | tf_op | source)
XLA Modules:
  0.0 970.8 jit_solution(2971991846381023970)
XLA Ops:
  8.1 1.1 convert_reduce_fusion.1
  9.2 1.2 fusion.73
  10.4 1.9 fusion.75
  12.4 1.4 copy.44
  13.8 42.5 %all-gather.7.cloned.1.call-done = bf16[1024,1024]{1,0:T(8,128)(2,1)} async-done(((bf16[128,1024]{1,0:T(8,128)(2,1)}), bf16[1024,1024]{1,0:T(8,128)(2,1)}) %all-gather.7.cloned.1.call-update) | async-done | bytes 2097168 | tf_op jit(solution)/shard_map/all_gather | solution.py:89
  56.3 2.6 convolution_convert_fusion.3
  58.9 4.9 fusion.97
  63.8 4.3 fusion.48
  68.1 2.1 convolution_convert_fusion.2
  71.9 39.8 %reduce-scatter.6.cloned.1.call-done = bf16[128,1024]{1,0:T(8,128)(2,1)} async-done(((bf16[1024,1024]{1,0:T(8,128)(2,1)}), bf16[128,1024]{1,0:T(8,128)(2,1)}) %reduce-scatter.6.cloned.1.call-update) | async-done | bytes 262160 | tf_op jit(solution)/shard_map/reduce_scatter | solution.py:92
  111.7 1.1 convert_reduce_fusion
  113.1 0.9 fusion.72
  114.1 18.6 %all-gather.11.cloned.1.call-done = bf16[1024,2,1024]{2,1,0:T(2,128)(2,1)} async-done(((bf16[64,2,1024]{2,1,0:T(2,128)(2,1)}), bf16[1024,2,1024]{2,1,0:T(2,128)(2,1)}) %all-gather.11.cloned.1.call-update) | async-done | bytes 4194320 | tf_op jit(solution)/shard_map/all_gather | solution.py:124
  132.7 11.1 %copy.47 = bf16[1024,2,1024]{0,2,1:T(8,128)(2,1)} copy(bf16[1024,2,1024]{2,1,0:T(2,128)(2,1)} %all-gather.11.cloned.1.call-done) | data formatting | bytes 8388608 | tf_op jit(solution)/shard_map/all_gather | solution.py:124
  143.8 4.6 convolution_convert_fusion
  148.5 39.0 %all-gather.15.cloned.1.call-done = bf16[1024,1024]{1,0:T(8,128)(2,1)} async-done(((bf16[64,1024]{1,0:T(8,128)(2,1)}), bf16[1024,1024]{1,0:T(8,128)(2,1)}) %all-gather.15.cloned.1.call-update) | async-done | bytes 2097168 | tf_op jit(solution)/shard_map/all_gather | solution.py:123
  187.5 2.3 convolution_convert_fusion.5
  189.8 1.0 copy.49
  190.8 51.5 %all-gather.17.cloned.1.call-done = bf16[1024,1024]{1,0:T(8,128)(2,1)} async-done(((bf16[64,1024]{1,0:T(8,128)(2,1)}), bf16[1024,1024]{1,0:T(8,128)(2,1)}) %all-gather.17.cloned.1.call-update) | async-done | bytes 2097168 | tf_op jit(solution)/shard_map/all_gather | solution.py:125
  242.3 2.3 convolution_convert_fusion.4
  244.6 1.0 copy.51
  245.6 39.2 %all-gather.9.cloned.1.call-done = bf16[1024,1024]{1,0:T(8,128)(2,1)} async-done(((bf16[128,1024]{1,0:T(8,128)(2,1)}), bf16[1024,1024]{1,0:T(8,128)(2,1)}) %all-gather.9.cloned.1.call-update) | async-done | bytes 2097168 | tf_op jit(solution)/shard_map/all_gather | solution.py:101
  284.9 5.8 convolution_convert_fusion.1
  290.9 66.3 %all-gather.13.cloned.1.call-done = bf16[1024,2048]{1,0:T(8,128)(2,1)} async-done(((bf16[128,2048]{1,0:T(8,128)(2,1)}), bf16[1024,2048]{1,0:T(8,128)(2,1)}) %all-gather.13.cloned.1.call-update) | async-done | bytes 4194320 | tf_op jit(solution)/shard_map/all_gather | solution.py:131
  357.2 4.0 fusion.96
  361.2 2.6 copy.50
  363.8 2.9 copy.48
  366.6 9.8 %fusion.98 = (f32[16,256]{1,0:T(8,128)S(1)}, f32[16,256,1024]{2,1,0:T(8,128)}) fusion(bf16[256,16,64]{0,2,1:T(8,128)(2,1)S(1)} %bitcast.149, bf16[1024,16,64]{0,2,1:T(8,128)(2,1)} %bitcast.144), kind=kOutput, calls=%fused_computation.110 | convolution fusion | flops 549454848 | bytes 19415040 | tf_op jit(solution)/shard_map/sub | solution.py:30
  376.5 8.1 fusion.99
  384.6 38.2 %fusion.38 = bf16[16,64,1024]{2,1,0:T(8,128)(2,1)} fusion(bf16[256,16,64]{0,2,1:T(8,128)(2,1)S(1)} %bitcast.150, f32[16,256,1024]{2,1,0:T(8,128)} %fusion.99, f32[16,256,1024]{2,1,0:T(8,128)} %get-tuple-element.18, f32[16,256]{1,0:T(8,128)S(1)} %get-tuple-element.17), kind=kOutput, calls=%fused_computation.40 | convolution fusion | flops 567284736 | bytes 36192256 | tf_op jit(solution)/shard_map/hrl,rhd->lhd/dot_general | solution.py:170
  422.7 7.1 fusion.35
  429.9 2.4 pad_maximum_fusion
  432.2 6.5 copy.57
  439.1 8.5 fusion.42
  447.6 2.7 fusion.78
  450.4 1.8 broadcast_select_fusion
  452.2 40.7 %reduce-scatter.10.cloned.1.call-done = bf16[128,2048]{1,0:T(8,128)(2,1)} async-done(((bf16[1024,2048]{1,0:T(8,128)(2,1)}), bf16[128,2048]{1,0:T(8,128)(2,1)}) %reduce-scatter.10.cloned.1.call-update) | async-done | bytes 524304
  492.9 2.1 copy.58
  495.0 104.4 %all-reduce.5.cloned.1.call-done = f32[1024,1024]{1,0:T(8,128)} async-done(((f32[1024,1024]{1,0:T(8,128)}), f32[1024,1024]{1,0:T(8,128)}) %all-reduce.5.cloned.1.call-update) | async-done | bytes 4194320 | tf_op jit(solution)/shard_map/psum | solution.py:161
  599.4 10.0 %fusion.95 = (bf16[1024,1,1024]{2,1,0:T(2,128)(2,1)}, bf16[1024,1,1024]{2,1,0:T(2,128)(2,1)}) fusion(bf16[1024,2,1024]{2,1,0:T(2,128)(2,1)} %all-gather.11.cloned.1.call-done), kind=kLoop, calls=%fused_computation.107 | loop fusion | bytes 8388608 | tf_op jit(solution)/shard_map/slice | solution.py:49
  609.4 1.9 collective-permute-start
  611.4 1.5 fusion.45
  612.9 7.1 collective-permute-done
  620.0 129.4 %all-reduce.9.cloned.1.call-done = (bf16[128,1024]{1,0:T(8,128)(2,1)}, bf16[128,2,1024]{0,2,1:T(8,128)(2,1)}) async-done(((bf16[128,1024]{1,0:T(8,128)(2,1)}, bf16[128,2,1024]{0,2,1:T(8,128)(2,1)}), (bf16[128,1024]{1,0:T(8,128)(2,1)}, bf16[128,2,1024]{0,2,1:T(8,128)(2,1)})) %all-reduce.9.cloned.1.call-update) | async-done | bytes 786448 | tf_op jit(solution)/shard_map/psum | solution.py:18
  750.9 3.1 fusion.33
  754.0 3.9 fusion.49
  757.9 200.3 %all-reduce.7.cloned.1.call-done = f32[1024,1024]{1,0:T(8,128)} async-done(((f32[1024,1024]{1,0:T(8,128)}), f32[1024,1024]{1,0:T(8,128)}) %all-reduce.7.cloned.1.call-update) | async-done | bytes 4194320 | tf_op jit(solution)/shard_map/psum | solution.py:161
  958.9 4.8 copy.77
  (61 shorter events, 5.2 us)
Async XLA Ops:
  8.0 276.9 %copy-start = (bf16[1,512,1024]{2,1,0:T(8,128)(2,1)S(1)}, bf16[1,512,1024]{2,1,0:T(8,128)(2,1)}, u32[]{:S(2)}) copy-start(bf16[1,512,1024]{2,1,0:T(8,128)(2,1)} %param.19) | copy-start | bytes 3145732
  8.0 48.2 %all-gather.7.cloned.1.call-start = ((), (), s32[]{:S(2)}) async-start(), calls=%async_computation.3 | async-start | bytes 2359296 | tf_op jit(solution)/shard_map/all_gather | solution.py:89
  12.3 99.4 %reduce-scatter.6.cloned.1.call-start = ((), (), s32[]{:S(2)}) async-start(), calls=%async_computation.4 | async-start | bytes 2359296 | tf_op jit(solution)/shard_map/reduce_scatter | solution.py:92
  63.7 4.3 copy-start.11
  68.0 43.7 %copy-start.2 = (bf16[1,1,128,1024]{3,2,1,0:T(8,128)(2,1)S(1)}, bf16[1,1,128,1024]{3,2,1,0:T(8,128)(2,1)}, u32[]{:S(2)}) copy-start(bf16[1,1,128,1024]{3,2,1,0:T(8,128)(2,1)} %param.13) | copy-start | bytes 786436
  68.0 45.0 %copy-start.13 = (f32[1,1024]{1,0:T(1,128)S(1)}, f32[1,1024]{1,0:T(1,128)}, u32[]{:S(2)}) copy-start(f32[1,1024]{1,0:T(1,128)} %param.17) | copy-start | bytes 12292
  70.1 62.5 %all-gather.11.cloned.1.call-start = ((), (), s32[]{:S(2)}) async-start(), calls=%async_computation.7 | async-start | bytes 4456448 | tf_op jit(solution)/shard_map/all_gather | solution.py:124
  70.7 116.8 %all-gather.15.cloned.1.call-start = ((), (), s32[]{:S(2)}) async-start(), calls=%async_computation.9 | async-start | bytes 2228224 | tf_op jit(solution)/shard_map/all_gather | solution.py:123
  71.3 171.0 %all-gather.17.cloned.1.call-start = ((), (), s32[]{:S(2)}) async-start(), calls=%async_computation.10 | async-start | bytes 2228224 | tf_op jit(solution)/shard_map/all_gather | solution.py:125
  71.9 213.0 %all-gather.9.cloned.1.call-start = ((), (), s32[]{:S(2)}) async-start(), calls=%async_computation.5 | async-start | bytes 2359296 | tf_op jit(solution)/shard_map/all_gather | solution.py:101
  114.0 29.8 %copy-start.12 = (bf16[1,128,1024]{2,1,0:T(8,128)(2,1)S(1)}, bf16[1,128,1024]{2,1,0:T(8,128)(2,1)}, u32[]{:S(2)}) copy-start(bf16[1,128,1024]{2,1,0:T(8,128)(2,1)} %param.20) | copy-start | bytes 786436
  114.0 243.2 %all-gather.13.cloned.1.call-start = ((), (), s32[]{:S(2)}) async-start(), calls=%async_computation.8 | async-start | bytes 4718592 | tf_op jit(solution)/shard_map/all_gather | solution.py:131
  143.8 43.7 %copy-start.8 = (bf16[1,256,1024]{2,1,0:T(8,128)(2,1)S(1)}, bf16[1,256,1024]{2,1,0:T(8,128)(2,1)}, u32[]{:S(2)}) copy-start(bf16[1,256,1024]{2,1,0:T(8,128)(2,1)} %param.21) | copy-start | bytes 1572868
  143.8 98.5 %copy-start.6 = (bf16[1,256,1024]{2,1,0:T(8,128)(2,1)S(1)}, bf16[1,256,1024]{2,1,0:T(8,128)(2,1)}, u32[]{:S(2)}) copy-start(bf16[1,256,1024]{2,1,0:T(8,128)(2,1)} %param.25) | copy-start | bytes 1572868
  148.4 302.0 %reduce-scatter.8.cloned.1.call-start = ((), (), s32[]{:S(2)}) async-start(), calls=%async_computation.6 | async-start | bytes 2359296 | tf_op jit(solution)/shard_map/reduce_scatter | solution.py:109
  290.7 202.2 %reduce-scatter.10.cloned.1.call-start = ((), (), s32[]{:S(2)}) async-start(), calls=%async_computation.13 | async-start | bytes 4718592
  361.2 5.4 copy-start.10
  366.6 9.8 %copy-start.4 = (bf16[256,1024]{0,1:T(8,128)(2,1)S(1)}, bf16[256,1024]{0,1:T(8,128)(2,1)}, u32[]{:S(2)}) copy-start(bf16[256,1024]{0,1:T(8,128)(2,1)} %copy.51) | copy-start | bytes 1572868
  422.7 7.1 copy-start.5
  438.8 8.8 copy-start.7
  438.8 160.6 %all-reduce.5.cloned.1.call-start = ((), (), s32[]{:S(2)}) async-start(), calls=%async_computation.11 | async-start | bytes 8388608 | tf_op jit(solution)/shard_map/psum | solution.py:161
  450.4 299.0 %all-reduce.9.cloned.1.call-start = ((), (), s32[]{:S(2)}) async-start(), calls=%async_computation.14 | async-start | bytes 1572864 | tf_op jit(solution)/shard_map/psum | solution.py:18
  495.0 463.3 %all-reduce.7.cloned.1.call-start = ((), (), s32[]{:S(2)}) async-start(), calls=%async_computation.12 | async-start | bytes 8388608 | tf_op jit(solution)/shard_map/psum | solution.py:161
  599.4 11.9 %copy-start.3 = (bf16[1024,1024]{1,0:T(8,128)(2,1)S(1)}, bf16[1024,1024]{1,0:T(8,128)(2,1)}, u32[]{:S(2)}) copy-start(bf16[1024,1024]{1,0:T(8,128)(2,1)} %all-gather.17.cloned.1.call-done) | copy-start | bytes 6291460
  599.4 11.9 %copy-start.9 = (bf16[1,256,1024]{2,1,0:T(8,128)(2,1)S(1)}, bf16[1,256,1024]{2,1,0:T(8,128)(2,1)}, u32[]{:S(2)}) copy-start(bf16[1,256,1024]{2,1,0:T(8,128)(2,1)} %param.21) | copy-start | bytes 1572868
  609.4 10.5 %collective-permute-start = (bf16[128,1024]{1,0:T(8,128)(2,1)S(1)}, bf16[128,1024]{1,0:T(8,128)(2,1)S(1)}, u32[]{:S(2)}, u32[]{:S(2)}) collective-permute-start(bf16[128,1024]{1,0:T(8,128)(2,1)S(1)} %get-tuple-element.8), channel_id=1, source_target_pairs={{0,16},{16,32},{32,48},{48,64},{64,80},{80,96},{96,112},{112,128},... | collective-permute-start | bytes 786440 | tf_op jit(solution)/shard_map/ppermute | solution.py:13
  958.2 5.5 copy-start.1
Sparse Core Ops, SparseCore 0:
  12.4 43.7 all-gather.6
  70.3 41.3 reduce-scatter.5
  290.8 69.1 reduce-scatter.7
  438.9 53.8 reduce-scatter.9
Sparse Core Ops, SparseCore 1:
  73.4 59.3 all-gather.10
  135.3 52.1 all-gather.14
  190.1 52.1 all-gather.16
  244.7 40.1 all-gather.8
  286.7 70.4 all-gather.12
  450.4 148.9 all-reduce.4
  602.5 146.7 all-reduce.8
  751.9 206.3 all-reduce.6
